TPU v7x, 32 devices: a whole 2x2x4 slice. The times are simulated.
32 devices in a mesh: prow: 8 (over z, core), pcol: 4 (over y, x).
Axes of the slice: x: 2, y: 2, z: 4, core: 2. Of those that a mesh axis runs over, the one named last changes fastest.
Arguments:
- diag_block: float32 [256, 256], P('prow', 'pcol'), as said below
- panel: float32 [16384, 256], P('prow', 'pcol'), may hold values from -1.5 to 1.5
- slab: float32 [16384, 1024], P('prow', 'pcol'), may hold values from -6 to 6
Outputs:
- diag_factor: float32 [256, 256], P('prow', 'pcol')
- panel_factor: float32 [16384, 256], P('prow', 'pcol')
- slab_updated: float32 [16384, 1024], P('prow', 'pcol')
Inputs may be any that keep to these rules, and one draw needn't show every extreme that they name: diag_block is symmetric positive definite.
All inputs are finite; a program needn't handle non-finite values.
Results may differ from a plain program's by a relative error of at most 0.0003.
Values sent between devices are 32-bit elements; how exact they have to be, the bound alone decides.
A program may use at most 64 MiB of HBM per device.

v0:
```python
import functools

import jax
import jax.numpy as jnp
from jax import lax
from jax.experimental import pallas as pl
from jax.experimental.pallas import tpu as pltpu
from jax.sharding import PartitionSpec as P

HI = lax.Precision.HIGHEST
F32 = jnp.float32
NB = 64
EARLY = 3
VMEM_LIMIT = 24 * 1024 * 1024
MESH = pl.DeviceIdType.MESH


def dot_hi(a, b):
    return jnp.dot(a, b, precision=HI, preferred_element_type=F32)


def small(groups, width, one):
    lanes = 2 * width
    sub = lax.broadcasted_iota(jnp.int32, (8, lanes), 0)
    eight = range(8)
    count = width // 8

    def spread(x):
        return jnp.broadcast_to(x, (8, lanes))

    def column(x, j):
        return spread(x[:, j : j + 1])

    for g0 in range(count):
        base, first = groups[g0], 8 * g0
        columns = [column(base, first + k) * one for k in eight]
        d = {(m, k): spread(columns[k][m : m + 1, :]) for k in eight for m in range(k, 8)}
        rows = [spread(base[k : k + 1, :]) for k in eight]
        after = groups[g0 + 1] if g0 + 1 < count else None
        ahead = [column(after, first + k) for k in eight] if after is not None else None
        scales = []
        for k in eight:
            scale = lax.rsqrt(d[k, k])
            scales.append(scale)
            for m in range(k + 1, 8):
                d[m, k] = d[m, k] * scale
            for m in range(k + 1, 8):
                for q in range(k + 1, m + 1):
                    d[m, q] = d[m, q] - d[m, k] * d[q, k]
            rows[k] = rows[k] * scale
            for m in range(k + 1, 8):
                rows[m] = rows[m] - d[m, k] * rows[k]
            if ahead is not None:
                ahead[k] = ahead[k] * scale
                for m in range(k + 1, 8):
                    ahead[m] = ahead[m] - d[m, k] * ahead[k]
                after = after - ahead[k] * rows[k]
        solved = rows[0]
        for k in range(1, 8):
            solved = jnp.where(sub == k, rows[k], solved)
        groups[g0] = solved
        if ahead is not None:
            groups[g0 + 1] = after
        if g0 + 2 < count:
            back = [None] * 8
            for k in reversed(eight):
                total = rows[k]
                for m in range(k + 1, 8):
                    total = total - d[m, k] * back[m]
                back[k] = total * scales[k]
            for g in range(g0 + 2, count):
                terms = [column(groups[g], first + k) * back[k] for k in eight]
                while len(terms) > 1:
                    terms = [x + y for x, y in zip(terms[::2], terms[1::2])]
                groups[g] = groups[g] - terms[0]
    return jnp.concatenate(groups, axis=0)


def factor_block(matrix, upper, inverse, size, b, one):
    start, end = b * NB, (b + 1) * NB
    eye = (
        lax.broadcasted_iota(jnp.int32, (NB, NB), 0)
        == lax.broadcasted_iota(jnp.int32, (NB, NB), 1)
    ).astype(F32)
    right = matrix[start:end, start:]
    if b:
        left = upper[:start, start:end].T
        right = right - dot_hi(left, upper[:start, start:])
    if b > 1:
        last = start - NB
        below = dot_hi(upper[:last, last:start].T, inverse[:last, :last])
        inverse[last:start, :last] = -dot_hi(inverse[last:start, last:start], below)
    if b and end == size:
        for i in range(b):
            for j in range(i + 1, b):
                inverse[i * NB : (i + 1) * NB, j * NB : (j + 1) * NB] = jnp.zeros((NB, NB), F32)
        below = dot_hi(left, inverse[:start, :start])
    both = jnp.concatenate([right[:, :NB], eye], axis=1)
    solved = small([both[8 * g : 8 * g + 8] for g in range(NB // 8)], NB, one)
    triangle = (
        lax.broadcasted_iota(jnp.int32, (NB, NB), 1)
        >= lax.broadcasted_iota(jnp.int32, (NB, NB), 0)
    )
    upper[start:end, start:end] = jnp.where(triangle, solved[:, :NB], 0.0)
    own = solved[:, NB:]
    inverse[start:end, start:end] = own
    if end < size:
        upper[start:end, end:] = dot_hi(own, right[:, NB:])
    elif b:
        inverse[start:end, :start] = -dot_hi(own, below)


def split(x):
    high = x.astype(jnp.bfloat16)
    return high, (x - high.astype(F32)).astype(jnp.bfloat16)


def dot_split(a, b):
    (ah, al), (bh, bl) = a, b
    dot = functools.partial(jnp.dot, preferred_element_type=F32)
    return dot(ah, bh) + (dot(ah, bl) + dot(al, bh))


def main_kernel(
    rows, cols, group, fold,
    diag, panel, slab,
    diag_out, panel_out, slab_out,
    diag_own, tiles, gathered, matrix, upper, inverse, lower, strip_all, solved,
    own_sem, tile_send, tile_recv, wide_send, wide_recv,
    panel_send, panel_recv, strip_send, strip_recv, swap_send, mate_send, mate_recv,
):
    row, col = lax.axis_index("prow"), lax.axis_index("pcol")
    high, low = diag.shape
    size = matrix.shape[0]
    width, local_rows = panel.shape
    blocks = local_rows // size
    relay = cols == 4 and blocks % 2 == 0

    def remote(src, dst, send, recv, to):
        return pltpu.make_async_remote_copy(
            src_ref=src, dst_ref=dst, send_sem=send, recv_sem=recv,
            device_id=to, device_id_type=MESH,
        )

    def down(d):
        return {"prow": lax.rem(row + d, rows)}

    def across(d):
        return {"pcol": lax.rem(col + d, cols)}

    barrier = pltpu.get_barrier_semaphore()
    for d in range(1, rows):
        pl.semaphore_signal(barrier, inc=1, device_id=down(d), device_id_type=MESH)
    for d in range(1, cols):
        pl.semaphore_signal(barrier, inc=1, device_id=across(d), device_id_type=MESH)
    load = pltpu.make_async_copy(diag, diag_own, own_sem.at[0])
    load.start()
    own_panel = pltpu.make_async_copy(panel, gathered.at[col], own_sem.at[1])
    own_panel.start()
    own_slab = pltpu.make_async_copy(slab, slab_out, own_sem.at[2])
    own_slab.start()
    load.wait()
    step = high // fold
    packed = [diag_own[p * step : (p + 1) * step, :] for p in range(fold)]
    packed = jnp.concatenate(packed, axis=1) if fold > 1 else packed[0]
    tiles[pl.ds(col, 1), pl.ds(row, 1)] = packed[None, None]
    pl.semaphore_wait(barrier, rows + cols - 2)

    def needed(c):
        return ((c * low) // NB + 1) * NB // high

    my_tile = tiles.at[col, row]
    tile_copies = [
        remote(my_tile, my_tile, tile_send.at[d], tile_recv.at[row], down(d)) for d in range(1, rows)
    ]

    @pl.when(row < needed(col))
    def _():
        for copy in tile_copies:
            copy.start()

    def unit(u):
        return pl.ds(pl.multiple_of(u * size, size), size)

    def panel_copy(slot, u, to):
        return remote(
            panel.at[:, unit(u)], gathered.at[col, :, unit(u)],
            panel_send.at[slot, u], panel_recv.at[slot, u], to,
        )

    def arrived(slot, u):
        panel_copy(slot, u, across(1)).wait_recv()

    wanted = [c * group // rows for c in range(cols)]
    my_wanted = col * group // rows
    if relay:
        side, other = col + 1 - 2 * lax.rem(col, 2), lax.rem(col + 2, 4)
        opposite = 3 - col
        to_side, to_other = {"pcol": side}, {"pcol": other}
        near, far = list(range(blocks // 2)), list(range(blocks // 2, blocks))

        def order(k, mine, rest, neighbour):
            first = [wanted[k ^ 3]] if wanted[k ^ 3] in mine else []
            return list(dict.fromkeys(first + [wanted[neighbour]] + mine + rest))

        side_order = [order(k, near, far, k ^ 1) for k in range(4)]
        other_order = [order(k, far, near, k ^ 2) for k in range(4)]
        side_relay = [[u for u in side_order[c ^ 1] if u in near] for c in range(4)]
        other_relay = [[u for u in other_order[c ^ 2] if u in far] for c in range(4)]
        steps = blocks // 2

        def own_units(low_step, high_step):
            for c in range(4):

                @pl.when(col == c)
                def _():
                    for j in range(low_step, high_step):
                        panel_copy(0, side_order[c][j], to_side).start()
                        panel_copy(1, other_order[c][j], to_other).start()

        def forward(source, u, to):
            view = gathered.at[source, :, unit(u)]
            return remote(view, view, panel_send.at[2, u], panel_recv.at[2, u], to)

        def relay_step(j, waited):
            for c in range(4):

                @pl.when(col == c)
                def _():
                    u, v = side_relay[c][j], other_relay[c][j]
                    if not (waited and u == wanted[c]):
                        arrived(0, u)
                    forward(side, u, to_other).start()
                    if not (waited and v == wanted[c]):
                        arrived(1, v)
                    forward(other, v, to_side).start()

        own_units(0, EARLY)
    else:
        for u in range(blocks):
            for d in range(1, cols):
                panel_copy(d, u, across(d)).start()

    my_root = lax.rem(col * group, rows)
    core = lax.rem(row, 2)
    mate = {"prow": row + 1 - 2 * core}
    is_root = row == my_root
    same_chip = row // 2 == my_root // 2

    def strip_copy(k, d, src):
        return remote(src, strip_all.at[k], strip_send.at[k, d], strip_recv.at[k], down(d))

    def strip_half(k):
        return (k * 2) // cols

    def strip_each(k, act):
        def body(d, carry):
            to = lax.rem(row + d, rows)

            @pl.when((to // 2 == row // 2) | (lax.rem(to, 2) == strip_half(k)))
            def _():
                act(d)

            return carry

        lax.fori_loop(1, rows, body, 0)

    def strip_give(k, src):
        strip_each(k, lambda d: strip_copy(k, d, src).start())

    def strip_view(k):
        return gathered.at[k, :, unit(my_wanted)]

    @pl.when(is_root)
    def _():
        strip_give(col, panel.at[:, unit(my_wanted)])

    for r in range(rows):

        @pl.when((row != r) & (r < needed(col)))
        def _():
            there = tiles.at[col, r]
            remote(there, there, tile_send.at[0], tile_recv.at[r], down(1)).wait_recv()

    def wide(c, d):
        half = needed(c) // 2
        view = tiles.at[c, pl.ds(core * half, half)]
        if d is None:
            return remote(view, view, mate_send.at[c], mate_recv.at[c], mate)
        return remote(view, view, wide_send.at[d], wide_recv.at[c], across(d))

    for c in range(cols):

        @pl.when(col == c)
        def _():
            for d in range(1, cols):
                wide(c, d).start()

    if relay:
        for c in range(4):

            @pl.when(col == c)
            def _():
                u, v = side_relay[c][0], other_relay[c][0]
                arrived(0, u)
                forward(side, u, to_other).start()
                arrived(1, v)
                forward(other, v, to_side).start()
                for j in range(EARLY, blocks):
                    panel_copy(0, side_order[c][j], to_side).start()
                    panel_copy(1, other_order[c][j], to_other).start()
                if wanted[c] != u:
                    arrived(0, wanted[c])
                if wanted[c] != v:
                    arrived(1, wanted[c])

        @pl.when(is_root)
        def _():
            strip_give(side, strip_view(side))
            strip_give(other, strip_view(other))
    for c in range(cols):

        @pl.when(col != c)
        def _():
            wide(c, 1).wait_recv()
            wide(c, None).start()

    for c in range(cols):

        @pl.when(col != c)
        def _():
            wide(c, None).wait_recv()

    if not relay:
        for d in range(1, cols):
            arrived(d, my_wanted)

        @pl.when(is_root)
        def _():
            for d in range(1, cols):
                source = lax.rem(col + cols - d, cols)
                strip_give(source, strip_view(source))

    for c in range(cols):
        for r in range(needed(c)):
            for p in range(fold):
                top = r * high + p * step
                matrix[top : top + step, c * low : (c + 1) * low] = tiles[c, r][
                    :, p * low : (p + 1) * low
                ]
    one = jnp.where(row < rows, 1.0, 0.0).astype(F32)

    def swap(k):
        view = strip_all.at[k]
        return remote(view, view, swap_send.at[k], strip_recv.at[k], mate)

    for b in range(size // NB):
        factor_block(matrix, upper, inverse, size, b, one)
        if relay:
            if b == 0:
                arrived(2, my_wanted)

                @pl.when(is_root)
                def _():
                    strip_give(opposite, strip_view(opposite))

            for j in range(1, steps):
                if min(j - 1, size // NB - 2) == b:
                    relay_step(j, True)
        if b >= size // NB - 2:

            @pl.when(jnp.logical_not(same_chip))
            def _():
                for k in range(cols):
                    late = k == cols - 1 - col
                    now = late if b == size // NB - 1 else jnp.logical_not(late)

                    @pl.when((core == strip_half(k)) & now)
                    def _():
                        swap(k).wait_recv()
                        swap(k).start()

    for i in range(size // NB - 1):
        inverse[i * NB : (i + 1) * NB, size - NB :] = jnp.zeros((NB, NB), F32)
    own_panel.wait()

    @pl.when(is_root)
    def _():
        own = pltpu.make_async_copy(gathered.at[:, :, unit(my_wanted)], strip_all, own_sem.at[3])
        own.start()
        own.wait()

    for k in range(cols):

        @pl.when(jnp.logical_not(is_root) & (same_chip | (core != strip_half(k))))
        def _():
            swap(k).wait_recv()

    strip = split(dot_hi(inverse[...], strip_all[...].reshape(size, size)))
    inverse_parts = split(inverse[...])
    own_slab.wait()

    def update(i):
        here = slice(i * size, (i + 1) * size)
        full = gathered[:, :, here].reshape(size, size)
        factor = dot_split(inverse_parts, split(full))
        solved[...] = factor
        panel_out[:, here] = solved[pl.ds(pl.multiple_of(col * low, low), low), :]
        product = dot_split(split(factor.T), strip)
        shift = (i * rows + row - col * group) * size
        shape = (size, slab.shape[1])
        keep = (
            lax.broadcasted_iota(jnp.int32, shape, 0) + shift
            >= lax.broadcasted_iota(jnp.int32, shape, 1)
        )
        before = slab_out[here, :]
        slab_out[here, :] = jnp.where(keep, before - product, before)

    def settle(i):
        @pl.when(my_wanted != i)
        def _():
            if relay:
                arrived(1 if i in near else 0, i)
                arrived(2, i)
            else:
                for d in range(1, cols):
                    arrived(d, i)

    def finish_diag():
        for i in range(size // NB):
            for j in range(i, size // NB):
                at_i, at_j = slice(i * NB, (i + 1) * NB), slice(j * NB, (j + 1) * NB)
                lower[at_j, at_i] = upper[at_i, at_j].T
                if j > i:
                    lower[at_i, at_j] = jnp.zeros((NB, NB), F32)
        for c in range(cols):

            @pl.when(col == c)
            def _():
                start = pl.multiple_of(row * high, high)
                diag_out[...] = lower[pl.ds(start, high), c * low : (c + 1) * low]

    def drain():
        @pl.when(row < needed(col))
        def _():
            for copy in tile_copies:
                copy.wait_send()

        for c in range(cols):

            @pl.when(col == c)
            def _():
                for d in range(1, cols):
                    wide(c, d).wait_send()

            @pl.when(col != c)
            def _():
                wide(c, None).wait_send()

        for slot in range(3) if relay else range(1, cols):
            for u in range(blocks):
                panel_copy(slot, u, across(1)).wait_send()

        @pl.when(is_root)
        def _():
            for k in range(cols):
                strip_each(k, lambda d: strip_copy(k, d, strip_all.at[k]).wait_send())

        @pl.when(jnp.logical_not(same_chip))
        def _():
            for k in range(cols):

                @pl.when(core == strip_half(k))
                def _():
                    swap(k).wait_send()

    if relay:
        for i, j in zip(near, far):
            if i == blocks // 2 - 1:
                finish_diag()
                drain()
            settle(i)
            settle(j)
            update(i)
            update(j)
    else:
        for i in range(blocks):
            settle(i)
            update(i)
        finish_diag()
        drain()


def store_kernel(diag, panel, slab, diag_out, panel_out, slab_out, sems):
    copies = [
        pltpu.make_async_copy(slab, slab_out, sems.at[0]),
        pltpu.make_async_copy(panel, panel_out, sems.at[1]),
        pltpu.make_async_copy(diag, diag_out, sems.at[2]),
    ]
    for copy in copies:
        copy.start()
    for copy in copies:
        copy.wait()


def local(rows, cols, diag_block, panel, slab):
    high, low = diag_block.shape
    size = high * rows
    local_rows, width = panel.shape
    blocks = local_rows // size
    group = blocks * rows // cols
    fold = 128 // low if low < 128 and high * low % 1024 == 0 else 1
    hbm = pl.BlockSpec(memory_space=pltpu.HBM)
    vmem = pl.BlockSpec(memory_space=pltpu.VMEM)
    dma = pltpu.SemaphoreType.DMA
    shapes = [
        jax.ShapeDtypeStruct(diag_block.shape, F32),
        jax.ShapeDtypeStruct((width, local_rows), F32),
        jax.ShapeDtypeStruct(slab.shape, F32),
    ]
    slots = max(cols, 3)
    results = pl.pallas_call(
        functools.partial(main_kernel, rows, cols, group, fold),
        out_shape=shapes,
        in_specs=[hbm, hbm, hbm],
        out_specs=[vmem, vmem, vmem],
        scratch_shapes=[
            pltpu.VMEM((high, low), F32),
            pltpu.VMEM((cols, rows, high // fold, low * fold), F32),
            pltpu.VMEM((cols, width, local_rows), F32),
            pltpu.VMEM((size, size), F32),
            pltpu.VMEM((size, size), F32),
            pltpu.VMEM((size, size), F32),
            pltpu.VMEM((size, size), F32),
            pltpu.VMEM((cols, width, size), F32),
            pltpu.VMEM((size, size), F32),
            dma((4,)), dma((rows,)), dma((rows,)), dma((cols,)), dma((cols,)),
            dma((slots, blocks)), dma((slots, blocks)),
            dma((cols, rows)), dma((cols,)), dma((cols,)), dma((cols,)), dma((cols,)),
        ],
        compiler_params=pltpu.CompilerParams(
            collective_id=0, has_side_effects=True, vmem_limit_bytes=VMEM_LIMIT
        ),
        name="gather_update",
    )(*[pltpu.with_memory_space_constraint(x, pltpu.HBM) for x in (diag_block, panel.T, slab)])
    diag_out, panel_out, slab_out = pl.pallas_call(
        store_kernel,
        out_shape=shapes,
        in_specs=[vmem, vmem, vmem],
        out_specs=[hbm, hbm, hbm],
        scratch_shapes=[dma((3,))],
        compiler_params=pltpu.CompilerParams(vmem_limit_bytes=VMEM_LIMIT),
        name="store",
    )(*results)
    return diag_out, panel_out.T, slab_out


def solution(mesh):
    spec = P("prow", "pcol")
    return jax.shard_map(
        functools.partial(local, mesh.shape["prow"], mesh.shape["pcol"]),
        mesh=mesh,
        in_specs=(spec, spec, spec),
        out_specs=(spec, spec, spec),
        check_vma=False,
    )
```

profile of v0, /device:TPU:0, one launch (start us, length us, event | category | flops | bytes accessed | tf_op | source)
XLA Modules:
  0.0 32.1 jit_solution(2246045618740237875)
XLA Ops:
  0.6 30.0 %gather_update.1 = (f32[32,64]{1,0:T(8,128)S(1)}, f32[64,2048]{1,0:T(8,128)S(1)}, f32[2048,256]{1,0:T(8,128)S(1)}) custom-call(f32[32,64]{1,0:T(8,128)} %diag.1, f32[64,2048]{1,0:T(8,128)} %bitcast.2, f32[2048,256]{1,0:T(8,128)} %slab.1), custom_call_target="tpu_custom_call" | custom-call | tf_op jit(solution)/shard_map/gather_update/pallas_call | solution.py:522
  30.6 1.5 %store.1 = (f32[32,64]{1,0:T(8,128)}, f32[64,2048]{1,0:T(8,128)}, f32[2048,256]{1,0:T(8,128)}) custom-call(f32[32,64]{1,0:T(8,128)S(1)} %get-tuple-element.9.diag, f32[64,2048]{1,0:T(8,128)S(1)} %get-tuple-element.10.panel, f32[2048,256]{1,0:T(8,128)S(1)} %get-tuple-element.11.slab), custom_call_target="tpu_custom_call" | custom-call | tf_op jit(solution)/shard_map/store/pallas_call | solution.py:546
where the time goes:
time: 32.3 us; the launch traced here: 32.1 us
  Pallas kernels  31.5 us (98%)
  between operations  0.64 us (2%)
    pallas_call x1, Pallas kernels, local(): pl.pallas_call(functools.partial(main_kernel, rows, cols, group, fold), o...  30 us
    pallas_call x1, Pallas kernels, local(): pl.pallas_call(store_kernel, out_shape=shapes, in_specs=[vmem, vmem, vmem...  1.51 us

commit v1 on v0

--- a/solution.py
+++ b/solution.py
@@ -19,7 +19,7 @@
     return jnp.dot(a, b, precision=HI, preferred_element_type=F32)
 
 
-def small(groups, width, one):
+def small(groups, width, one, midway):
     lanes = 2 * width
     sub = lax.broadcasted_iota(jnp.int32, (8, lanes), 0)
     eight = range(8)
@@ -32,6 +32,8 @@
         return spread(x[:, j : j + 1])
 
     for g0 in range(count):
+        if g0 == count // 2:
+            midway()
         base, first = groups[g0], 8 * g0
         columns = [column(base, first + k) * one for k in eight]
         d = {(m, k): spread(columns[k][m : m + 1, :]) for k in eight for m in range(k, 8)}
@@ -76,7 +78,7 @@
     return jnp.concatenate(groups, axis=0)
 
 
-def factor_block(matrix, upper, inverse, size, b, one):
+def factor_block(matrix, upper, inverse, below, size, b, one, midway):
     start, end = b * NB, (b + 1) * NB
     eye = (
         lax.broadcasted_iota(jnp.int32, (NB, NB), 0)
@@ -88,15 +90,15 @@
         right = right - dot_hi(left, upper[:start, start:])
     if b > 1:
         last = start - NB
-        below = dot_hi(upper[:last, last:start].T, inverse[:last, :last])
-        inverse[last:start, :last] = -dot_hi(inverse[last:start, last:start], below)
+        sums = dot_hi(upper[:last, last:start].T, inverse[:last, :last])
+        inverse[last:start, :last] = -dot_hi(inverse[last:start, last:start], sums)
     if b and end == size:
         for i in range(b):
             for j in range(i + 1, b):
                 inverse[i * NB : (i + 1) * NB, j * NB : (j + 1) * NB] = jnp.zeros((NB, NB), F32)
-        below = dot_hi(left, inverse[:start, :start])
+        below[:, :start] = dot_hi(left, inverse[:start, :start])
     both = jnp.concatenate([right[:, :NB], eye], axis=1)
-    solved = small([both[8 * g : 8 * g + 8] for g in range(NB // 8)], NB, one)
+    solved = small([both[8 * g : 8 * g + 8] for g in range(NB // 8)], NB, one, midway)
     triangle = (
         lax.broadcasted_iota(jnp.int32, (NB, NB), 1)
         >= lax.broadcasted_iota(jnp.int32, (NB, NB), 0)
@@ -107,7 +109,7 @@
     if end < size:
         upper[start:end, end:] = dot_hi(own, right[:, NB:])
     elif b:
-        inverse[start:end, :start] = -dot_hi(own, below)
+        inverse[start:end, :start] = -dot_hi(own, below[:, :start])
 
 
 def split(x):
@@ -125,7 +127,7 @@
     rows, cols, group, fold,
     diag, panel, slab,
     diag_out, panel_out, slab_out,
-    diag_own, tiles, gathered, matrix, upper, inverse, lower, strip_all, solved,
+    diag_own, tiles, gathered, matrix, upper, inverse, lower, strip_all, below,
     own_sem, tile_send, tile_recv, wide_send, wide_recv,
     panel_send, panel_recv, strip_send, strip_recv, swap_send, mate_send, mate_recv,
 ):
@@ -348,37 +350,50 @@
                 matrix[top : top + step, c * low : (c + 1) * low] = tiles[c, r][
                     :, p * low : (p + 1) * low
                 ]
+    if relay and steps > 1:
+        relay_step(1, True)
     one = jnp.where(row < rows, 1.0, 0.0).astype(F32)
 
     def swap(k):
         view = strip_all.at[k]
         return remote(view, view, swap_send.at[k], strip_recv.at[k], mate)
 
-    for b in range(size // NB):
-        factor_block(matrix, upper, inverse, size, b, one)
-        if relay:
-            if b == 0:
-                arrived(2, my_wanted)
-
-                @pl.when(is_root)
+    last = size // NB - 1
+
+    def swap_part(final):
+        @pl.when(jnp.logical_not(same_chip))
+        def _():
+            for k in range(cols):
+                late = k == cols - 1 - col
+
+                @pl.when((core == strip_half(k)) & (late if final else jnp.logical_not(late)))
                 def _():
-                    strip_give(opposite, strip_view(opposite))
-
-            for j in range(1, steps):
-                if min(j - 1, size // NB - 2) == b:
+                    swap(k).wait_recv()
+                    swap(k).start()
+
+    def midway(b):
+        if b == last:
+            swap_part(True)
+        elif b == last - 1:
+            swap_part(False)
+        elif relay and b > 0:
+            for j in range(3, steps):
+                if min(j - 2, last - 2) == b:
                     relay_step(j, True)
-        if b >= size // NB - 2:
-
-            @pl.when(jnp.logical_not(same_chip))
+
+    for b in range(last + 1):
+        factor_block(
+            matrix, upper, inverse, below, size, b, one, functools.partial(midway, b)
+        )
+        if relay and b == 0:
+            arrived(2, my_wanted)
+
+            @pl.when(is_root)
             def _():
-                for k in range(cols):
-                    late = k == cols - 1 - col
-                    now = late if b == size // NB - 1 else jnp.logical_not(late)
-
-                    @pl.when((core == strip_half(k)) & now)
-                    def _():
-                        swap(k).wait_recv()
-                        swap(k).start()
+                strip_give(opposite, strip_view(opposite))
+
+            if steps > 2:
+                relay_step(2, True)
 
     for i in range(size // NB - 1):
         inverse[i * NB : (i + 1) * NB, size - NB :] = jnp.zeros((NB, NB), F32)
@@ -396,17 +411,16 @@
         def _():
             swap(k).wait_recv()
 
-    strip = split(dot_hi(inverse[...], strip_all[...].reshape(size, size)))
-    inverse_parts = split(inverse[...])
+    whole = inverse[...]
+    strip = split(dot_hi(whole.T, dot_hi(whole, strip_all[...].reshape(size, size))))
+    own_rows = split(inverse[pl.ds(pl.multiple_of(col * low, low), low), :])
     own_slab.wait()
 
     def update(i):
         here = slice(i * size, (i + 1) * size)
         full = gathered[:, :, here].reshape(size, size)
-        factor = dot_split(inverse_parts, split(full))
-        solved[...] = factor
-        panel_out[:, here] = solved[pl.ds(pl.multiple_of(col * low, low), low), :]
-        product = dot_split(split(factor.T), strip)
+        panel_out[:, here] = dot_split(own_rows, split(full))
+        product = dot_split(split(full.T), strip)
         shift = (i * rows + row - col * group) * size
         shape = (size, slab.shape[1])
         keep = (
@@ -533,7 +547,7 @@
             pltpu.VMEM((size, size), F32),
             pltpu.VMEM((size, size), F32),
             pltpu.VMEM((cols, width, size), F32),
-            pltpu.VMEM((size, size), F32),
+            pltpu.VMEM((NB, size), F32),
             dma((4,)), dma((rows,)), dma((rows,)), dma((cols,)), dma((cols,)),
             dma((slots, blocks)), dma((slots, blocks)),
             dma((cols, rows)), dma((cols,)), dma((cols,)), dma((cols,)), dma((cols,)),

time: 32.3 us -> 30.8 us (0.954)
  Pallas kernels: 31.5 us -> 30 us
    pallas_call x1, Pallas kernels: 30 us -> 28.5 us  [local(): pl.pallas_call(functools.partial(main_kernel, rows, cols, group, fold), o...]
where the time goes in v1:
time: 30.8 us; the launch traced here: 30.6 us
  Pallas kernels  30 us (97%)
  between operations  0.64 us (2%)
    pallas_call x1, Pallas kernels, local(): pl.pallas_call(functools.partial(main_kernel, rows, cols, group, fold), o...  28.5 us
    pallas_call x1, Pallas kernels, local(): pl.pallas_call(store_kernel, out_shape=shapes, in_specs=[vmem, vmem, vmem...  1.51 us

profile of v1, /device:TPU:0, one launch (start us, length us, event | category | flops | bytes accessed | tf_op | source)
XLA Modules:
  0.0 30.6 jit_solution(532944113516664959)
XLA Ops:
  0.6 28.5 %gather_update.1 = (f32[32,64]{1,0:T(8,128)S(1)}, f32[64,2048]{1,0:T(8,128)S(1)}, f32[2048,256]{1,0:T(8,128)S(1)}) custom-call(f32[32,64]{1,0:T(8,128)} %diag.1, f32[64,2048]{1,0:T(8,128)} %bitcast.2, f32[2048,256]{1,0:T(8,128)} %slab.1), custom_call_target="tpu_custom_call" | custom-call | tf_op jit(solution)/shard_map/gather_update/pallas_call | solution.py:536
  29.1 1.5 %store.1 = (f32[32,64]{1,0:T(8,128)}, f32[64,2048]{1,0:T(8,128)}, f32[2048,256]{1,0:T(8,128)}) custom-call(f32[32,64]{1,0:T(8,128)S(1)} %get-tuple-element.9.diag, f32[64,2048]{1,0:T(8,128)S(1)} %get-tuple-element.10.panel, f32[2048,256]{1,0:T(8,128)S(1)} %get-tuple-element.11.slab), custom_call_target="tpu_custom_call" | custom-call | tf_op jit(solution)/shard_map/store/pallas_call | solution.py:560
